TPU v7x, 32 devices: a whole 2x2x4 slice. The times are simulated.
32 devices in a mesh: ens: 4 (over y, x), space: 8 (over z, core).
Axes of the slice: x: 2, y: 2, z: 4, core: 2. Of those that a mesh axis runs over, the one named last changes fastest.
Arguments:
- latent: bfloat16 [16, 256, 8192], P('ens', None, 'space'), may hold values from -6 to 6
- noise: bfloat16 [16, 256, 8192], P('ens', None, 'space'), may hold values from -6 to 6
- target: float32 [224, 8192], P('ens', 'space'), may hold values from -6 to 6
- w_in: bfloat16 [384, 256], replicated, may hold values from -0.375 to 0.375
- w_out: bfloat16 [224, 384], replicated, may hold values from -0.3125 to 0.3125
- w_close_in: bfloat16 [384, 224], replicated, may hold values from -0.375 to 0.375
- w_close_out: bfloat16 [224, 384], replicated, may hold values from -0.3125 to 0.3125
Outputs:
- grad_latent: float32 [16, 256, 8192], P('ens', None, 'space')
- step_in: float32 [384, 256], replicated
- step_out: float32 [224, 384], replicated
- step_close_in: float32 [384, 224], replicated
- step_close_out: float32 [224, 384], replicated
All inputs are finite; a program needn't handle non-finite values.
Results may differ from a plain program's by a relative error of at most 0.011.
Values sent between devices are 32-bit elements; how exact they have to be, the bound alone decides.
A program may use at most 128 MiB of HBM per device.

v0:
```python
import jax
import jax.numpy as jnp
from jax import lax
from jax.sharding import PartitionSpec as P

smooth_eps = 0.1


def activate(value):
    return jax.nn.gelu(value, approximate=True)


def activate_back(pre, grad):
    return jax.vjp(activate, pre)[1](grad)[0]


def smooth_sign(diff):
    return diff / jnp.sqrt(diff * diff + smooth_eps * smooth_eps)


def pair_terms(mine, every, truth):
    count = every.shape[0]

    def add_one(index, total):
        other = lax.dynamic_index_in_dim(every, index, 0, keepdims=False)
        return total + smooth_sign(mine - other)

    total = lax.fori_loop(0, count, add_one, jnp.zeros_like(mine))
    return smooth_sign(mine - truth) - total / count


def body(latent, noise, target, w_in, w_out, w_close_in, w_close_out):
    f32 = jnp.float32
    zin = (latent.astype(f32) + 0.5 * noise.astype(f32)).astype(jnp.bfloat16)
    pre1 = jnp.einsum("hf,mfc->mhc", w_in, zin, preferred_element_type=f32)
    hid1 = activate(pre1).astype(jnp.bfloat16)
    dec = jnp.einsum("kh,mhc->mkc", w_out, hid1, preferred_element_type=f32)
    decb = dec.astype(jnp.bfloat16)
    pre3 = jnp.einsum("hk,mkc->mhc", w_close_in, decb, preferred_element_type=f32)
    hid3 = activate(pre3).astype(jnp.bfloat16)
    pred = dec + jnp.einsum("kh,mhc->mkc", w_close_out, hid3, preferred_element_type=f32)
    every, full_target = (
        lax.all_gather(pred, "ens", axis=0, tiled=True),
        lax.all_gather(target, "ens", axis=0, tiled=True),
    )
    gpred = pair_terms(pred, every, full_target)
    gpredb = gpred.astype(jnp.bfloat16)
    g_close_out = jnp.einsum("mkc,mhc->kh", gpredb, hid3, preferred_element_type=f32)
    g_hid3 = jnp.einsum("kh,mkc->mhc", w_close_out, gpredb, preferred_element_type=f32)
    gpre3 = activate_back(pre3, g_hid3).astype(jnp.bfloat16)
    g_close_in = jnp.einsum("mhc,mkc->hk", gpre3, decb, preferred_element_type=f32)
    gdec = (
        gpred + jnp.einsum("hk,mhc->mkc", w_close_in, gpre3, preferred_element_type=f32)
    ).astype(jnp.bfloat16)
    g_out = jnp.einsum("mkc,mhc->kh", gdec, hid1, preferred_element_type=f32)
    g_hid1 = jnp.einsum("kh,mkc->mhc", w_out, gdec, preferred_element_type=f32)
    gpre1 = activate_back(pre1, g_hid1).astype(jnp.bfloat16)
    g_in = jnp.einsum("mhc,mfc->hf", gpre1, zin, preferred_element_type=f32)
    grad_latent = jnp.einsum("hf,mhc->mfc", w_in, gpre1, preferred_element_type=f32)
    g_in, g_out, g_close_in, g_close_out = lax.psum(
        (g_in, g_out, g_close_in, g_close_out), ("ens", "space")
    )
    count = g_in.size + g_out.size + g_close_in.size + g_close_out.size
    squares = (
        jnp.sum(g_in * g_in)
        + jnp.sum(g_out * g_out)
        + jnp.sum(g_close_in * g_close_in)
        + jnp.sum(g_close_out * g_close_out)
    )
    rms = jnp.sqrt(squares / count + 1e-12)
    return (grad_latent, g_in / rms, g_out / rms, g_close_in / rms, g_close_out / rms)


def solution(mesh):
    placed = (
        P("ens", None, "space"),
        P("ens", None, "space"),
        P("ens", "space"),
        P(),
        P(),
        P(),
        P(),
    )
    return jax.shard_map(
        body,
        mesh=mesh,
        in_specs=placed,
        out_specs=(P("ens", None, "space"), P(), P(), P(), P()),
        check_vma=False,
    )
```

profile of v0, /device:TPU:0, one launch (start us, length us, event | category | flops | bytes accessed | tf_op | source)
XLA Modules:
  0.0 469.2 jit_solution(4322245571807078582)
XLA Ops:
  25.6 14.1 %all_gather.6 = f32[224,1024]{1,0:T(8,128)S(1)} all-gather(f32[56,1024]{1,0:T(8,128)S(1)} %copy-done.8), channel_id=1, replica_groups=mesh['ens'=4,'space'=8] {'ens'}, dimensions={0}, use_global_device_ids=true | all-gather | bytes 1146880 | tf_op jit(solution)/shard_map/all_gather | solution.py:44
  39.7 128.7 %all-gather.2.cloned.1.call-done = f32[16,224,1024]{2,1,0:T(8,128)} async-done(((f32[4,224,1024]{2,1,0:T(8,128)}), f32[16,224,1024]{2,1,0:T(8,128)}) %all-gather.2.cloned.1.call-update) | async-done | bytes 14680080 | tf_op jit(solution)/shard_map/all_gather | solution.py:43
  168.3 120.0 %while.14 = (s32[]{:T(128)}, f32[4,224,1024]{2,1,0:T(8,128)}, f32[16,224,1024]{2,1,0:T(8,128)}, f32[4,224,1024]{2,1,0:T(8,128)}, s32[]{:T(128)}, /*index=5*/s32[]{:T(128)}) while((s32[]{:T(128)}, f32[4,224,1024]{2,1,0:T(8,128)}, f32[16,224,1024]{2,1,0:T(8,128)}, f32[4,224,1024]{2,1,0:T(8,128)}, s32[]{:T(128)}, ...), condition=%wide.region_1.2_spmd.clone, body=%wide.region_0.1_spmd.clone.sunk | while | flops 5505027 | bytes 13762643 | solution.py:28
  169.6 5.2 %select_add_fusion.2 = f32[4,224,1024]{2,1,0:T(8,128)} fusion(f32[4,224,1024]{2,1,0:T(8,128)} %get-tuple-element.156, f32[4,224,1024]{2,1,0:T(8,128)} %get-tuple-element.164, f32[224,1024]{1,0:T(8,128)S(1)} %dynamic-slice_bitcast_fusion.2, pred[]{:T(512)S(6)} %compare.3), kind=kLoop, calls=%fused_computation.clone.1 | loop fusion | flops 5505024 | bytes 11927553 | tf_op jit(solution)/shard_map/while/body/eval_jaxpr/add | solution.py:26
  176.0 6.3 %select_add_fusion.2 = f32[4,224,1024]{2,1,0:T(8,128)} fusion(f32[4,224,1024]{2,1,0:T(8,128)} %get-tuple-element.156, f32[4,224,1024]{2,1,0:T(8,128)} %get-tuple-element.164, f32[224,1024]{1,0:T(8,128)S(1)} %dynamic-slice_bitcast_fusion.2, pred[]{:T(512)S(6)} %compare.3), kind=kLoop, calls=%fused_computation.clone.1 | loop fusion | flops 5505024 | bytes 11927553 | tf_op jit(solution)/shard_map/while/body/eval_jaxpr/add | solution.py:26
  183.6 6.3 %select_add_fusion.2 = f32[4,224,1024]{2,1,0:T(8,128)} fusion(f32[4,224,1024]{2,1,0:T(8,128)} %get-tuple-element.156, f32[4,224,1024]{2,1,0:T(8,128)} %get-tuple-element.164, f32[224,1024]{1,0:T(8,128)S(1)} %dynamic-slice_bitcast_fusion.2, pred[]{:T(512)S(6)} %compare.3), kind=kLoop, calls=%fused_computation.clone.1 | loop fusion | flops 5505024 | bytes 11927553 | tf_op jit(solution)/shard_map/while/body/eval_jaxpr/add | solution.py:26
  191.2 6.3 %select_add_fusion.2 = f32[4,224,1024]{2,1,0:T(8,128)} fusion(f32[4,224,1024]{2,1,0:T(8,128)} %get-tuple-element.156, f32[4,224,1024]{2,1,0:T(8,128)} %get-tuple-element.164, f32[224,1024]{1,0:T(8,128)S(1)} %dynamic-slice_bitcast_fusion.2, pred[]{:T(512)S(6)} %compare.3), kind=kLoop, calls=%fused_computation.clone.1 | loop fusion | flops 5505024 | bytes 11927553 | tf_op jit(solution)/shard_map/while/body/eval_jaxpr/add | solution.py:26
  198.7 6.3 %select_add_fusion.2 = f32[4,224,1024]{2,1,0:T(8,128)} fusion(f32[4,224,1024]{2,1,0:T(8,128)} %get-tuple-element.156, f32[4,224,1024]{2,1,0:T(8,128)} %get-tuple-element.164, f32[224,1024]{1,0:T(8,128)S(1)} %dynamic-slice_bitcast_fusion.2, pred[]{:T(512)S(6)} %compare.3), kind=kLoop, calls=%fused_computation.clone.1 | loop fusion | flops 5505024 | bytes 11927553 | tf_op jit(solution)/shard_map/while/body/eval_jaxpr/add | solution.py:26
  206.3 6.3 %select_add_fusion.2 = f32[4,224,1024]{2,1,0:T(8,128)} fusion(f32[4,224,1024]{2,1,0:T(8,128)} %get-tuple-element.156, f32[4,224,1024]{2,1,0:T(8,128)} %get-tuple-element.164, f32[224,1024]{1,0:T(8,128)S(1)} %dynamic-slice_bitcast_fusion.2, pred[]{:T(512)S(6)} %compare.3), kind=kLoop, calls=%fused_computation.clone.1 | loop fusion | flops 5505024 | bytes 11927553 | tf_op jit(solution)/shard_map/while/body/eval_jaxpr/add | solution.py:26
  213.9 6.3 %select_add_fusion.2 = f32[4,224,1024]{2,1,0:T(8,128)} fusion(f32[4,224,1024]{2,1,0:T(8,128)} %get-tuple-element.156, f32[4,224,1024]{2,1,0:T(8,128)} %get-tuple-element.164, f32[224,1024]{1,0:T(8,128)S(1)} %dynamic-slice_bitcast_fusion.2, pred[]{:T(512)S(6)} %compare.3), kind=kLoop, calls=%fused_computation.clone.1 | loop fusion | flops 5505024 | bytes 11927553 | tf_op jit(solution)/shard_map/while/body/eval_jaxpr/add | solution.py:26
  221.4 6.3 %select_add_fusion.2 = f32[4,224,1024]{2,1,0:T(8,128)} fusion(f32[4,224,1024]{2,1,0:T(8,128)} %get-tuple-element.156, f32[4,224,1024]{2,1,0:T(8,128)} %get-tuple-element.164, f32[224,1024]{1,0:T(8,128)S(1)} %dynamic-slice_bitcast_fusion.2, pred[]{:T(512)S(6)} %compare.3), kind=kLoop, calls=%fused_computation.clone.1 | loop fusion | flops 5505024 | bytes 11927553 | tf_op jit(solution)/shard_map/while/body/eval_jaxpr/add | solution.py:26
  229.0 6.3 %select_add_fusion.2 = f32[4,224,1024]{2,1,0:T(8,128)} fusion(f32[4,224,1024]{2,1,0:T(8,128)} %get-tuple-element.156, f32[4,224,1024]{2,1,0:T(8,128)} %get-tuple-element.164, f32[224,1024]{1,0:T(8,128)S(1)} %dynamic-slice_bitcast_fusion.2, pred[]{:T(512)S(6)} %compare.3), kind=kLoop, calls=%fused_computation.clone.1 | loop fusion | flops 5505024 | bytes 11927553 | tf_op jit(solution)/shard_map/while/body/eval_jaxpr/add | solution.py:26
  236.6 6.3 %select_add_fusion.2 = f32[4,224,1024]{2,1,0:T(8,128)} fusion(f32[4,224,1024]{2,1,0:T(8,128)} %get-tuple-element.156, f32[4,224,1024]{2,1,0:T(8,128)} %get-tuple-element.164, f32[224,1024]{1,0:T(8,128)S(1)} %dynamic-slice_bitcast_fusion.2, pred[]{:T(512)S(6)} %compare.3), kind=kLoop, calls=%fused_computation.clone.1 | loop fusion | flops 5505024 | bytes 11927553 | tf_op jit(solution)/shard_map/while/body/eval_jaxpr/add | solution.py:26
  244.2 6.3 %select_add_fusion.2 = f32[4,224,1024]{2,1,0:T(8,128)} fusion(f32[4,224,1024]{2,1,0:T(8,128)} %get-tuple-element.156, f32[4,224,1024]{2,1,0:T(8,128)} %get-tuple-element.164, f32[224,1024]{1,0:T(8,128)S(1)} %dynamic-slice_bitcast_fusion.2, pred[]{:T(512)S(6)} %compare.3), kind=kLoop, calls=%fused_computation.clone.1 | loop fusion | flops 5505024 | bytes 11927553 | tf_op jit(solution)/shard_map/while/body/eval_jaxpr/add | solution.py:26
  251.7 6.3 %select_add_fusion.2 = f32[4,224,1024]{2,1,0:T(8,128)} fusion(f32[4,224,1024]{2,1,0:T(8,128)} %get-tuple-element.156, f32[4,224,1024]{2,1,0:T(8,128)} %get-tuple-element.164, f32[224,1024]{1,0:T(8,128)S(1)} %dynamic-slice_bitcast_fusion.2, pred[]{:T(512)S(6)} %compare.3), kind=kLoop, calls=%fused_computation.clone.1 | loop fusion | flops 5505024 | bytes 11927553 | tf_op jit(solution)/shard_map/while/body/eval_jaxpr/add | solution.py:26
  259.3 6.3 %select_add_fusion.2 = f32[4,224,1024]{2,1,0:T(8,128)} fusion(f32[4,224,1024]{2,1,0:T(8,128)} %get-tuple-element.156, f32[4,224,1024]{2,1,0:T(8,128)} %get-tuple-element.164, f32[224,1024]{1,0:T(8,128)S(1)} %dynamic-slice_bitcast_fusion.2, pred[]{:T(512)S(6)} %compare.3), kind=kLoop, calls=%fused_computation.clone.1 | loop fusion | flops 5505024 | bytes 11927553 | tf_op jit(solution)/shard_map/while/body/eval_jaxpr/add | solution.py:26
  266.9 6.3 %select_add_fusion.2 = f32[4,224,1024]{2,1,0:T(8,128)} fusion(f32[4,224,1024]{2,1,0:T(8,128)} %get-tuple-element.156, f32[4,224,1024]{2,1,0:T(8,128)} %get-tuple-element.164, f32[224,1024]{1,0:T(8,128)S(1)} %dynamic-slice_bitcast_fusion.2, pred[]{:T(512)S(6)} %compare.3), kind=kLoop, calls=%fused_computation.clone.1 | loop fusion | flops 5505024 | bytes 11927553 | tf_op jit(solution)/shard_map/while/body/eval_jaxpr/add | solution.py:26
  274.4 6.3 %select_add_fusion.2 = f32[4,224,1024]{2,1,0:T(8,128)} fusion(f32[4,224,1024]{2,1,0:T(8,128)} %get-tuple-element.156, f32[4,224,1024]{2,1,0:T(8,128)} %get-tuple-element.164, f32[224,1024]{1,0:T(8,128)S(1)} %dynamic-slice_bitcast_fusion.2, pred[]{:T(512)S(6)} %compare.3), kind=kLoop, calls=%fused_computation.clone.1 | loop fusion | flops 5505024 | bytes 11927553 | tf_op jit(solution)/shard_map/while/body/eval_jaxpr/add | solution.py:26
  282.0 6.3 %select_add_fusion.2 = f32[4,224,1024]{2,1,0:T(8,128)} fusion(f32[4,224,1024]{2,1,0:T(8,128)} %get-tuple-element.156, f32[4,224,1024]{2,1,0:T(8,128)} %get-tuple-element.164, f32[224,1024]{1,0:T(8,128)S(1)} %dynamic-slice_bitcast_fusion.2, pred[]{:T(512)S(6)} %compare.3), kind=kLoop, calls=%fused_computation.clone.1 | loop fusion | flops 5505024 | bytes 11927553 | tf_op jit(solution)/shard_map/while/body/eval_jaxpr/add | solution.py:26
  288.3 4.3 multiply_subtract_fusion
  293.3 4.8 %fusion.13 = bf16[4,384,1024]{1,2,0:T(8,128)(2,1)S(1)} fusion(f32[4,1024,384]{2,1,0:T(8,128)S(1)} %bitcast.110, f32[4,224,1024]{2,1,0:T(8,128)S(1)} %multiply_subtract_fusion, bf16[224,384]{1,0:T(8,128)(2,1)S(1)} %copy-done.9), kind=kOutput, calls=%fused_computation.19 | convolution fusion | flops 737017856 | bytes 13279232 | tf_op jit(solution)/shard_map/kh,mkc->mhc/dot_general | solution.py:49
  302.7 5.0 %fusion.6 = bf16[4,384,1024]{1,2,0:T(8,128)(2,1)S(1)} fusion(f32[4,1024,384]{2,1,0:T(8,128)S(1)} %bitcast.112, bf16[4,224,1024]{2,1,0:T(8,128)(2,1)S(1)} %fusion.22, bf16[224,384]{1,0:T(8,128)(2,1)S(1)} %copy-done.10), kind=kOutput, calls=%fused_computation.12 | convolution fusion | flops 736100352 | bytes 11444224 | tf_op jit(solution)/shard_map/kh,mkc->mhc/dot_general | solution.py:56
  317.9 5.4 %copy.29 = f32[4,256,1024]{2,1,0:T(8,128)} copy(f32[4,256,1024]{1,2,0:T(8,128)} %convolution_bitcast_fusion) | data formatting | bytes 8388608
  323.2 124.4 %all-reduce.3.cloned.1.call-done = (f32[384,256]{1,0:T(8,128)}, f32[224,384]{1,0:T(8,128)}, f32[384,224]{0,1:T(8,128)}, f32[224,384]{1,0:T(8,128)}) async-done(((f32[384,256]{1,0:T(8,128)}, f32[224,384]{1,0:T(8,128)}, f32[384,224]{0,1:T(8,128)}, f32[224,384]{1,0:T(8,128)}), (f32[384,256]{1,0:T(8,128)}, f32[224,384]{1,0:T(8,128)}, f32[384,224]{0,1:T(8,128)}, ...) | async-done | bytes 1425424 | tf_op jit(solution)/shard_map/psum | solution.py:60
  (70 shorter events, 65.5 us)
Async XLA Ops:
  7.2 0.9 copy-start
  7.2 7.0 %copy-start.10 = (bf16[224,384]{1,0:T(8,128)(2,1)S(1)}, bf16[224,384]{1,0:T(8,128)(2,1)}, u32[]{:S(2)}) copy-start(bf16[224,384]{1,0:T(8,128)(2,1)} %param.13) | copy-start | bytes 516100
  7.2 161.1 %all-gather.2.cloned.1.call-start = ((), (), s32[]{:S(2)}) async-start(), calls=%async_computation | async-start | bytes 18350080 | tf_op jit(solution)/shard_map/all_gather | solution.py:43
  11.6 2.6 copy-start.4
  14.2 2.7 copy-start.7
  16.9 1.9 copy-start.1
  16.9 4.5 copy-start.9
  18.8 2.7 copy-start.3
  21.5 4.1 copy-start.8
  25.5 422.1 %all-reduce.3.cloned.1.call-start = ((), (), s32[]{:S(2)}) async-start(), calls=%async_computation.1 | async-start | bytes 2850816 | tf_op jit(solution)/shard_map/psum | solution.py:60
  288.3 4.4 slice-start
  288.3 5.0 %slice-start.1 = ((s8[6291456]{0:T(1024)(128)(4,1)}), s8[2097152]{0:T(1024)(128)(4,1)S(1)}, s32[]{:S(2)}) async-start(s8[6291456]{0:T(1024)(128)(4,1)} %bitcast.109), calls=%async_computation.3 | async-start | bytes 4194304
  288.3 11.1 %slice-start.2 = ((s8[6291456]{0:T(1024)(128)(4,1)}), s8[4194304]{0:T(1024)(128)(4,1)S(1)}, s32[]{:S(2)}) async-start(s8[6291456]{0:T(1024)(128)(4,1)} %bitcast.111), calls=%async_computation.4 | async-start | bytes 8388608
  293.3 6.1 %slice-start.3 = ((s8[6291456]{0:T(1024)(128)(4,1)}), s8[2097152]{0:T(1024)(128)(4,1)S(1)}, s32[]{:S(2)}) async-start(s8[6291456]{0:T(1024)(128)(4,1)} %bitcast.111), calls=%async_computation.5 | async-start | bytes 4194304
  302.7 5.0 %copy-start.2 = (f32[4,1024,224]{1,2,0:T(8,128)S(1)}, f32[4,1024,224]{1,2,0:T(8,128)}, u32[]{:S(2)}) copy-start(f32[4,1024,224]{1,2,0:T(8,128)} %copy-done.1) | copy-start | bytes 11010052
  309.6 3.2 copy-start.5
  309.6 3.2 copy-start.6
Sparse Core Ops, SparseCore 0:
  25.6 142.6 all-gather.1
  314.8 132.7 all-reduce.2
where the time goes:
time: 470 us; the launch traced here: 469 us
  waiting for transfers between devices  253 us (54%)
  other arithmetic  116 us (25%)
  matrix products  36 us (8%)
  local copies, waits for them, and re-layouts  32.5 us (7%)
  between operations  16.8 us (4%)
  blocking collectives  14.1 us (3%)
    all_gather x1, waiting for transfers between devices, body(): lax.all_gather(pred, 'ens', axis=0, tiled=True)  129 us
    psum x1, waiting for transfers between devices, body(): lax.psum((g_in, g_out, g_close_in, g_close_out), ('ens', 'space'))  124 us
    add x16, other arithmetic, add_one(): return total + smooth_sign(mine - other)  100 us
    sub x16, local copies, waits for them, and re-layouts, add_one(): return total + smooth_sign(mine - other)  19.8 us
    all_gather x1, blocking collectives, body(): lax.all_gather(target, 'ens', axis=0, tiled=True)  14.1 us
    unnamed x31, local copies, waits for them, and re-layouts  12.7 us
  transfers between devices with their start and end apart: 2, of which 2 were waited for; matrix products, arithmetic and copies ran while one was open for 2% of the time, Pallas kernels for 0%

commit v1 on v0

v1 whole, which is shorter than its diff:
```python
import functools

import jax
import jax.numpy as jnp
from jax import lax
from jax.experimental import pallas as pl
from jax.experimental.pallas import tpu as pltpu
from jax.sharding import PartitionSpec as P

MESH = pl.DeviceIdType.MESH
EPS2 = 0.1 * 0.1
C0 = 0.7978845608028654
C1 = C0 * 0.044715
LANES = 128
F32 = jnp.float32
BF16 = jnp.bfloat16


def smooth_sign(diff):
    return diff * lax.rsqrt(diff * diff + EPS2)


def gelu_both(x):
    x2 = x * x
    t = jnp.tanh(x * (C0 + C1 * x2))
    half = 0.5 * x
    value = half + half * t
    slope = 0.5 + 0.5 * t + half * (1.0 - t * t) * (C0 + (3.0 * C1) * x2)
    return value, slope


def mm(a, b):
    return lax.dot_general(a, b, (((1,), (0,)), ((), ())), preferred_element_type=F32)


def mm_nt(a, b):
    return lax.dot_general(a, b, (((1,), (1,)), ((), ())), preferred_element_type=F32)


def step_kernel(
    ens,
    lat,
    noi,
    tgt,
    w_in,
    w_out,
    w_ci,
    w_co,
    w_in_t,
    w_out_t,
    w_ci_t,
    w_co_t,
    glat,
    gpack,
    zin_s,
    hid1_s,
    hid3_s,
    slope1_s,
    slope3_s,
    decb_s,
    out_pred,
    all_pred,
    out_grad,
    all_grad,
    t_in,
    t_all,
    gw_in,
    gw_out,
    gw_cit,
    gw_co,
    t_send,
    t_recv,
    p_send,
    p_recv,
    g_send,
    g_recv,
):
    members, fin, columns = lat.shape
    k = w_out.shape[0]
    rows_t = tgt.shape[0]
    share = columns // ens
    halves = share // LANES
    me = lax.axis_index("ens")
    sp = lax.axis_index("space")

    barrier = pltpu.get_barrier_semaphore()
    for t in range(1, ens):
        pl.semaphore_signal(
            barrier, inc=1, device_id=(lax.rem(me + t, ens), sp), device_id_type=MESH
        )
    pl.semaphore_wait(barrier, ens - 1)

    def target_copy(dst, src):
        return pltpu.make_async_remote_copy(
            src_ref=tgt.at[:, pl.ds(pl.multiple_of(dst * share, LANES), share)],
            dst_ref=t_in.at[src],
            send_sem=t_send.at[dst],
            recv_sem=t_recv.at[src],
            device_id=(dst, sp),
            device_id_type=MESH,
        )

    def pred_copy(h, dst, src):
        return pltpu.make_async_remote_copy(
            src_ref=out_pred.at[h, dst],
            dst_ref=all_pred.at[h, src],
            send_sem=p_send.at[h, dst],
            recv_sem=p_recv.at[h, src],
            device_id=(dst, sp),
            device_id_type=MESH,
        )

    def grad_copy(h, dst, src):
        return pltpu.make_async_remote_copy(
            src_ref=out_grad.at[h, dst],
            dst_ref=all_grad.at[h, src],
            send_sem=g_send.at[h, dst],
            recv_sem=g_recv.at[h, src],
            device_id=(dst, sp),
            device_id_type=MESH,
        )

    def forward(h, q):
        start = pl.multiple_of(q * share + h * LANES, LANES)
        cols = pl.ds(start, LANES)
        zin = jnp.concatenate(
            [
                (lat[m, :, cols].astype(F32) + 0.5 * noi[m, :, cols].astype(F32)).astype(BF16)
                for m in range(members)
            ],
            axis=1,
        )
        zin_s[h, q] = zin
        value, slope = gelu_both(mm(w_in[...], zin))
        hid1 = value.astype(BF16)
        hid1_s[h, q] = hid1
        slope1_s[h, q] = slope.astype(BF16)
        dec = mm(w_out[...], hid1)
        decb = dec.astype(BF16)
        decb_s[h, q] = decb
        value, slope = gelu_both(mm(w_ci[...], decb))
        hid3 = value.astype(BF16)
        hid3_s[h, q] = hid3
        slope3_s[h, q] = slope.astype(BF16)
        pred = dec + mm(w_co[...], hid3)
        for m in range(members):
            out_pred[h, q, m] = pred[:, m * LANES : (m + 1) * LANES]

    def pairs(h):
        count = ens * members

        def strip(r, carry):
            rows = pl.ds(pl.multiple_of(r * 8, 8), 8)
            x = [all_pred[h, i // members, i % members, rows, :] for i in range(count)]
            acc = [None] * count
            for i in range(count):
                for j in range(i + 1, count):
                    s = smooth_sign(x[i] - x[j])
                    acc[i] = s if acc[i] is None else acc[i] + s
                    acc[j] = -s if acc[j] is None else acc[j] - s
            truth = t_all[rows, h * LANES : (h + 1) * LANES]
            for i in range(count):
                out_grad[h, i // members, i % members, rows, :] = (
                    smooth_sign(x[i] - truth) - acc[i] * (1.0 / count)
                )
            return carry

        lax.fori_loop(0, k // 8, strip, 0)

    def backward(h, q):
        gp = jnp.concatenate([all_grad[h, q, m] for m in range(members)], axis=1)
        gpb = gp.astype(BF16)
        gw_co[...] += mm_nt(gpb, hid3_s[h, q])
        gpre3 = (slope3_s[h, q].astype(F32) * mm(w_co_t[...], gpb)).astype(BF16)
        gw_cit[...] += mm_nt(decb_s[h, q], gpre3)
        gdec = (gp + mm(w_ci_t[...], gpre3)).astype(BF16)
        gw_out[...] += mm_nt(gdec, hid1_s[h, q])
        gpre1 = (slope1_s[h, q].astype(F32) * mm(w_out_t[...], gdec)).astype(BF16)
        gw_in[...] += mm_nt(gpre1, zin_s[h, q])
        gl = mm(w_in_t[...], gpre1)
        cols = pl.ds(pl.multiple_of(q * share + h * LANES, LANES), LANES)
        for m in range(members):
            glat[m, :, cols] = gl[:, m * LANES : (m + 1) * LANES]

    for t in range(1, ens):
        target_copy(lax.rem(me + t, ens), me).start()
    t_in[me] = tgt[:, pl.ds(pl.multiple_of(me * share, LANES), share)]

    for h in range(halves):

        def go(t, carry, h=h):
            q = lax.rem(me + t, ens)
            forward(h, q)
            pred_copy(h, q, me).start()
            return carry

        lax.fori_loop(1, ens, go, 0)
        forward(h, me)
        all_pred[h, me] = out_pred[h, me]

    gw_in[...] = jnp.zeros_like(gw_in)
    gw_out[...] = jnp.zeros_like(gw_out)
    gw_cit[...] = jnp.zeros_like(gw_cit)
    gw_co[...] = jnp.zeros_like(gw_co)

    for t in range(1, ens):
        target_copy(lax.rem(me + t, ens), lax.rem(me + t, ens)).wait_recv()
    for e in range(ens):
        t_all[e * rows_t : (e + 1) * rows_t, :] = t_in[e]

    for h in range(halves):
        for t in range(1, ens):
            pred_copy(h, lax.rem(me + t, ens), lax.rem(me + t, ens)).wait_recv()
        pairs(h)
        for t in range(1, ens):
            grad_copy(h, lax.rem(me + t, ens), me).start()
        all_grad[h, me] = out_grad[h, me]

    for h in range(halves):

        def back(t, carry, h=h):
            q = lax.rem(me + t, ens)

            @pl.when(t > 0)
            def _():
                grad_copy(h, q, q).wait_recv()

            backward(h, q)
            return carry

        lax.fori_loop(0, ens, back, 0)

    for t in range(1, ens):
        target_copy(lax.rem(me + t, ens), me).wait_send()
        for h in range(halves):
            pred_copy(h, lax.rem(me + t, ens), me).wait_send()
            grad_copy(h, lax.rem(me + t, ens), me).wait_send()

    row = 0
    for ref in (gw_in, gw_out, gw_cit, gw_co):
        height, width = ref.shape
        for c in range(width // LANES):
            gpack[row : row + height, :] = ref[:, c * LANES : (c + 1) * LANES]
            row += height
    gpack[row:, :] = jnp.zeros((gpack.shape[0] - row, LANES), F32)


def reduce_kernel(
    ens,
    space,
    shapes,
    g,
    *refs,
):
    outs = refs[:4]
    part1, got1, part2, got2, got3, full, s1, r1, s2, r2, s3, r3, s4, r4, s5, r5, s6, r6 = refs[4:]
    rows = g.shape[0]
    half = rows // 2
    quarter = half // ens
    depth = space // 2
    piece = quarter // depth
    me = lax.axis_index("ens")
    sp = lax.axis_index("space")
    core = lax.rem(sp, 2)
    z = sp // 2
    mate = (me, sp + 1 - 2 * core)

    def at(start, size):
        return pl.ds(pl.multiple_of(start, 8), size)

    def ens_dev(e):
        return (e, sp)

    def z_dev(zz):
        return (me, zz * 2 + core)

    barrier = pltpu.get_barrier_semaphore()
    pl.semaphore_signal(barrier, inc=1, device_id=mate, device_id_type=MESH)
    for t in range(1, ens):
        pl.semaphore_signal(
            barrier, inc=1, device_id=ens_dev(lax.rem(me + t, ens)), device_id_type=MESH
        )
    for t in range(1, depth):
        pl.semaphore_signal(
            barrier, inc=1, device_id=z_dev(lax.rem(z + t, depth)), device_id_type=MESH
        )
    pl.semaphore_wait(barrier, 1 + (ens - 1) + (depth - 1))

    def copy(src, dst, send, recv, dev):
        return pltpu.make_async_remote_copy(
            src_ref=src, dst_ref=dst, send_sem=send, recv_sem=recv, device_id=dev, device_id_type=MESH
        )

    c1 = copy(g.at[at((1 - core) * half, half)], got1, s1.at[0], r1.at[0], mate)
    c1.start()
    c1.wait()
    part1[...] = g[at(core * half, half), :] + got1[...]

    def rs_ens(dst, src):
        return copy(part1.at[at(dst * quarter, quarter)], got2.at[src], s2.at[dst], r2.at[src], ens_dev(dst))

    for t in range(1, ens):
        rs_ens(lax.rem(me + t, ens), me).start()
    for t in range(1, ens):
        other = lax.rem(me + t, ens)
        rs_ens(other, other).wait_recv()
    total = part1[at(me * quarter, quarter), :]
    for t in range(1, ens):
        total = total + got2[lax.rem(me + t, ens)]
    part2[...] = total

    def rs_z(dst, src):
        return copy(part2.at[at(dst * piece, piece)], got3.at[src], s3.at[dst], r3.at[src], z_dev(dst))

    for t in range(1, depth):
        rs_z(lax.rem(z + t, depth), z).start()
    for t in range(1, depth):
        other = lax.rem(z + t, depth)
        rs_z(other, other).wait_recv()
    total = part2[at(z * piece, piece), :]
    for t in range(1, depth):
        total = total + got3[lax.rem(z + t, depth)]
    base = core * half + me * quarter
    full[at(base + z * piece, piece), :] = total

    def ag_z(dst, src):
        region = full.at[at(base + src * piece, piece)]
        return copy(region, region, s4.at[dst], r4.at[src], z_dev(dst))

    for t in range(1, depth):
        ag_z(lax.rem(z + t, depth), z).start()
    for t in range(1, depth):
        other = lax.rem(z + t, depth)
        ag_z(other, other).wait_recv()

    def ag_ens(dst, src):
        region = full.at[at(core * half + src * quarter, quarter)]
        return copy(region, region, s5.at[dst], r5.at[src], ens_dev(dst))

    for t in range(1, ens):
        ag_ens(lax.rem(me + t, ens), me).start()
    for t in range(1, ens):
        other = lax.rem(me + t, ens)
        ag_ens(other, other).wait_recv()

    mine = full.at[at(core * half, half)]
    c6 = copy(mine, mine, s6.at[0], r6.at[0], mate)
    c6.start()
    theirs = full.at[at((1 - core) * half, half)]
    copy(theirs, theirs, s6.at[0], r6.at[0], mate).wait_recv()

    c6.wait_send()
    for t in range(1, ens):
        other = lax.rem(me + t, ens)
        rs_ens(other, me).wait_send()
        ag_ens(other, me).wait_send()
    for t in range(1, depth):
        other = lax.rem(z + t, depth)
        rs_z(other, z).wait_send()
        ag_z(other, z).wait_send()

    used = sum(a * b for a, b in shapes) // LANES
    values = full[:used, :]
    squares = jnp.sum(values * values, keepdims=True)
    inverse = 1.0 / jnp.sqrt(squares / (used * LANES) + 1e-12)
    row = 0
    for out, (height, width) in zip(outs, shapes):
        for c in range(width // LANES):
            out[:, c * LANES : (c + 1) * LANES] = full[row : row + height, :] * inverse
            row += height


def body(ens, space, latent, noise, target, w_in, w_out, w_ci, w_co):
    members, fin, columns = latent.shape
    hid = w_in.shape[0]
    k = w_out.shape[0]
    rows_t = target.shape[0]
    share = columns // ens
    halves = share // LANES
    wide = members * LANES
    shapes = ((hid, fin), (k, hid), (k, hid), (k, hid))
    used = sum(a * b for a, b in shapes) // LANES
    unit = 8 * ens * space
    rows = -(-used // unit) * unit
    vmem = pl.BlockSpec(memory_space=pltpu.VMEM)
    dma = pltpu.SemaphoreType.DMA
    flops = 6 * 4 * hid * k * members * columns

    glat, gpack = pl.pallas_call(
        functools.partial(step_kernel, ens),
        name="crps_step",
        out_shape=(
            jax.ShapeDtypeStruct((members, fin, columns), F32),
            jax.ShapeDtypeStruct((rows, LANES), F32),
        ),
        in_specs=[vmem] * 11,
        out_specs=(vmem, vmem),
        scratch_shapes=[
            pltpu.VMEM((halves, ens, fin, wide), BF16),
            pltpu.VMEM((halves, ens, hid, wide), BF16),
            pltpu.VMEM((halves, ens, hid, wide), BF16),
            pltpu.VMEM((halves, ens, hid, wide), BF16),
            pltpu.VMEM((halves, ens, hid, wide), BF16),
            pltpu.VMEM((halves, ens, k, wide), BF16),
            pltpu.VMEM((halves, ens, members, k, LANES), F32),
            pltpu.VMEM((halves, ens, members, k, LANES), F32),
            pltpu.VMEM((halves, ens, members, k, LANES), F32),
            pltpu.VMEM((halves, ens, members, k, LANES), F32),
            pltpu.VMEM((ens, rows_t, share), F32),
            pltpu.VMEM((k, share), F32),
            pltpu.VMEM((hid, fin), F32),
            pltpu.VMEM((k, hid), F32),
            pltpu.VMEM((k, hid), F32),
            pltpu.VMEM((k, hid), F32),
            dma((ens,)),
            dma((ens,)),
            dma((halves, ens)),
            dma((halves, ens)),
            dma((halves, ens)),
            dma((halves, ens)),
        ],
        compiler_params=pltpu.CompilerParams(
            collective_id=0, has_side_effects=True, vmem_limit_bytes=58 * 2**20
        ),
        cost_estimate=pl.CostEstimate(flops=flops, bytes_accessed=2**24, transcendentals=2**24),
    )(latent, noise, target, w_in, w_out, w_ci, w_co, w_in.T, w_out.T, w_ci.T, w_co.T)

    half = rows // 2
    quarter = half // ens
    depth = space // 2
    piece = quarter // depth
    s_in, s_out, s_cit, s_co = pl.pallas_call(
        functools.partial(reduce_kernel, ens, space, shapes),
        name="weight_sum",
        out_shape=tuple(jax.ShapeDtypeStruct(s, F32) for s in shapes),
        in_specs=[vmem],
        out_specs=(vmem,) * 4,
        scratch_shapes=[
            pltpu.VMEM((half, LANES), F32),
            pltpu.VMEM((half, LANES), F32),
            pltpu.VMEM((quarter, LANES), F32),
            pltpu.VMEM((ens, quarter, LANES), F32),
            pltpu.VMEM((depth, piece, LANES), F32),
            pltpu.VMEM((rows, LANES), F32),
            dma((1,)),
            dma((1,)),
            dma((ens,)),
            dma((ens,)),
            dma((depth,)),
            dma((depth,)),
            dma((depth,)),
            dma((depth,)),
            dma((ens,)),
            dma((ens,)),
            dma((1,)),
            dma((1,)),
        ],
        compiler_params=pltpu.CompilerParams(
            collective_id=1, has_side_effects=True, vmem_limit_bytes=32 * 2**20
        ),
    )(gpack)
    return glat, s_in, s_out, s_cit.T, s_co


def solution(mesh):
    placed = (
        P("ens", None, "space"),
        P("ens", None, "space"),
        P("ens", "space"),
        P(),
        P(),
        P(),
        P(),
    )
    return jax.shard_map(
        functools.partial(body, mesh.shape["ens"], mesh.shape["space"]),
        mesh=mesh,
        in_specs=placed,
        out_specs=(P("ens", None, "space"), P(), P(), P(), P()),
        check_vma=False,
    )
```

time: 470 us -> 149 us (0.32)
  waiting for transfers between devices: 253 us -> 0 us
  Pallas kernels: 0 us -> 132 us
  other arithmetic: 116 us -> 0 us
  matrix products: 36 us -> 0 us
  local copies, waits for them, and re-layouts: 32.5 us -> 16 us
  between operations: 16.8 us -> 0.66 us
  blocking collectives: 14.1 us -> 0 us
    pallas_call x0 -> x2, Pallas kernels: none -> 132 us  [the longest x1 95.7 us: body(): pl.pallas_call(functools.partial(step_kernel, ens), name='crps_step', out...]
    all_gather x1 -> x0, waiting for transfers between devices: 129 us -> none  [body(): lax.all_gather(pred, 'ens', axis=0, tiled=True)]
    psum x1 -> x0, waiting for transfers between devices: 124 us -> none  [body(): lax.psum((g_in, g_out, g_close_in, g_close_out), ('ens', 'space'))]
    add x16 -> x0, other arithmetic: 100 us -> none  [add_one(): return total + smooth_sign(mine - other)]
    dot_general x12 -> x0, matrix products: 36 us -> none  [the longest x1 5.03 us: body(): g_hid1 = jnp.einsum('kh,mkc->mhc', w_out, gdec, preferred_element_type=f32)]
    sub x16 -> x0, local copies, waits for them, and re-layouts: 19.8 us -> none  [add_one(): return total + smooth_sign(mine - other)]
    all_gather x1 -> x0, blocking collectives: 14.1 us -> none  [body(): lax.all_gather(target, 'ens', axis=0, tiled=True)]
    div x4 -> x0, other arithmetic: 6.98 us -> none  [the longest x1 1.77 us: body(): g_in / rms]
  transfers between devices with their start and end apart: 2 -> 0, of which waited for: 2 -> 0; matrix products, arithmetic and copies ran while one was open for 2% -> 0% of each run, Pallas kernels for 0% -> 0%
where the time goes in v1:
time: 149 us
  Pallas kernels  132 us (89%)
  local copies, waits for them, and re-layouts  16 us (11%)
    pallas_call x1, Pallas kernels, body(): pl.pallas_call(functools.partial(step_kernel, ens), name='crps_step', out...  95.7 us
    pallas_call x1, Pallas kernels, body(): pl.pallas_call(functools.partial(reduce_kernel, ens, space, shapes), name...  36.5 us
    unnamed x11, local copies, waits for them, and re-layouts  16 us

profile of v1, /device:TPU:0, one launch (start us, length us, event | category | flops | bytes accessed | tf_op | source)
XLA Modules:
  0.0 148.9 jit_solution(1483212540792021702)
XLA Ops:
  0.6 1.7 %copy.12 = bf16[384,256]{0,1:T(8,128)(2,1)} copy(bf16[384,256]{1,0:T(8,128)(2,1)} %w_in.1) | data formatting | bytes 393216 | tf_op args[3]
  2.4 1.7 %copy.13 = bf16[224,384]{0,1:T(8,128)(2,1)} copy(bf16[224,384]{1,0:T(8,128)(2,1)} %w_out.1) | data formatting | bytes 344064 | tf_op args[4]
  4.1 1.7 %copy.14 = bf16[224,384]{0,1:T(8,128)(2,1)} copy(bf16[224,384]{1,0:T(8,128)(2,1)} %w_co.1) | data formatting | bytes 344064 | tf_op args[6]
  5.8 1.7 %copy.15.w_ci = bf16[384,224]{1,0:T(8,128)(2,1)} copy(bf16[384,224]{0,1:T(8,128)(2,1)} %param.12) | data formatting | bytes 344064 | tf_op args[5]
  7.6 95.7 %crps_step.1 = (f32[4,256,1024]{2,1,0:T(8,128)}, f32[2816,128]{1,0:T(8,128)}) custom-call(bf16[4,256,1024]{2,1,0:T(8,128)(2,1)} %lat.1, bf16[4,256,1024]{2,1,0:T(8,128)(2,1)} %noi.1, f32[56,1024]{1,0:T(8,128)} %tgt.1, bf16[384,256]{1,0:T(8,128)(2,1)} %w_in.1, bf16[224,384]{1,0:T(8,128)(2,1)} %w_out.1, bf16[384,224]{1,0:T(8,128)(2,1)} %copy.15.w_ci, ...), custom_call_target="tpu_custom_call" | custom-call | flops 8455716864 | bytes 16777216 | tf_op jit(solution)/shard_map/crps_step/pallas_call | solution.py:389
  103.3 0.0 copy-start
  103.3 1.4 copy-done
  104.6 36.5 %weight_sum.1 = (f32[384,256]{1,0:T(8,128)S(1)}, f32[224,384]{1,0:T(8,128)S(1)}, f32[224,384]{1,0:T(8,128)S(1)}, f32[224,384]{1,0:T(8,128)S(1)}) custom-call(f32[2816,128]{1,0:T(8,128)S(1)} %copy-done), custom_call_target="tpu_custom_call" | custom-call | tf_op jit(solution)/shard_map/weight_sum/pallas_call | solution.py:432
  141.1 4.8 %copy.21 = f32[4,256,1024]{2,1,0:T(8,128)} copy(f32[4,256,1024]{2,1,0:T(8,128)} %get-tuple-element.22) | data formatting | bytes 8388608
  145.9 0.7 copy.22
  146.7 0.7 copy.23
  147.4 0.7 copy.24
  148.1 0.7 copy.25
Async XLA Ops:
  103.3 1.4 copy-start
